TPU v7x, 256 devices: a whole 4x4x8 slice. The times are simulated.
256 devices in a mesh: dp: 64 (over z, y, core), tensor: 4 (over x).
Axes of the slice: x: 4, y: 4, z: 8, core: 2. Of those that a mesh axis runs over, the one named last changes fastest.
Arguments:
- queries: bfloat16 [32768, 2048], P('dp', 'tensor'), may hold values from -360 to 360
- neighbours: int32 [512, 2], P('dp'), may hold values from 0 to 63, as said below
- counts: int32 [512], P('dp'), may hold values from 1 to 2
- states: bfloat16 [64, 128, 4096], P('dp'), may hold values from -6 to 6
- w_key: bfloat16 [4096, 2048], P('dp', 'tensor'), may hold values from -0.09375 to 0.09375
- w_value: bfloat16 [4096, 2048], P('dp', 'tensor'), may hold values from -0.09375 to 0.09375
- cotangent: bfloat16 [32768, 2048], P('dp', 'tensor'), may hold values from -6 to 6
Outputs:
- context: bfloat16 [32768, 2048], P('dp', 'tensor')
- query_grad: bfloat16 [32768, 2048], P('dp', 'tensor')
- state_grad: bfloat16 [64, 128, 4096], P('dp', None, 'tensor')
Inputs may be any that keep to these rules, and one draw needn't show every extreme that they name: Neighbour n is held by dp index n. Among the 16 slots of one index of dp, at most 1 name neighbours of one holder, and some holder is named exactly 1 times.
All inputs are finite; a program needn't handle non-finite values.
Results may differ from a plain program's by a relative error of at most 0.035.
The roundings to bfloat16 on the way count: a program that leaves them out, or rounds other values in their place, can miss the bound.
Values may be sent and summed in bfloat16 or wider, within the bound.
A program may use at most 128 MiB of HBM per device.

v0:
```python
import math
import jax
import jax.numpy as jnp
from jax import lax
from jax.sharding import PartitionSpec as P

HEAD = 128


def local(queries, neighbours, counts, states, w_key, w_value, cotangent):
    dp_count = lax.axis_size("dp")
    spans, neigh = neighbours.shape
    slots = spans * neigh
    capacity = (slots + dp_count - 1) // dp_count
    buffer_rows = dp_count * capacity
    nbr_dev, nbr_len, dmodel = states.shape
    local_width = queries.shape[1]
    heads_here = local_width // HEAD
    span_len = queries.shape[0] // spans
    score_scale = 1.0 / math.sqrt(HEAD)
    slot_ids = neighbours.reshape(slots)
    holder = slot_ids // nbr_dev
    slot_order = jnp.arange(slots, dtype=jnp.int32)
    earlier = (holder[:, None] == holder[None, :]) & (slot_order[None, :] < slot_order[:, None])
    holder_rank = jnp.sum(earlier.astype(jnp.int32), axis=1)
    position = holder * capacity + holder_rank
    placing = position[None, :] == jnp.arange(buffer_rows, dtype=jnp.int32)[:, None]
    place_half = placing.astype(jnp.bfloat16)
    place_full = placing.astype(jnp.float32)
    query_spans = queries.reshape(spans, 1, span_len * local_width)
    query_slots = jnp.broadcast_to(query_spans, (spans, neigh, span_len * local_width)).reshape(
        slots, span_len * local_width
    )
    send_query = jnp.dot(place_half, query_slots, preferred_element_type=jnp.float32).astype(
        jnp.bfloat16
    )
    send_query = send_query.reshape(dp_count, capacity, span_len, local_width)
    flat_states = states.reshape(nbr_dev * nbr_len, dmodel)
    key_full = lax.all_gather(w_key, "dp", axis=0, tiled=True)
    value_full = lax.all_gather(w_value, "dp", axis=0, tiled=True)
    key_acc = jnp.dot(flat_states, key_full, preferred_element_type=jnp.float32)
    value_acc = jnp.dot(flat_states, value_full, preferred_element_type=jnp.float32)
    key_rows = key_acc.astype(jnp.bfloat16).reshape(nbr_len, heads_here, HEAD)
    value_rows = value_acc.astype(jnp.bfloat16).reshape(nbr_len, heads_here, HEAD)
    key_rows, value_rows, key_full, value_full = (key_rows, value_rows, key_full, value_full)
    recv_query = lax.all_to_all(send_query, "dp", split_axis=0, concat_axis=0, tiled=True)
    lead = recv_query.shape[:-1]
    item_query = recv_query.reshape(lead + (heads_here, HEAD))
    scores = (
        jnp.einsum("abqhd,khd->abqhk", item_query, key_rows, preferred_element_type=jnp.float32)
        * score_scale
    )
    row_max = jnp.max(scores, axis=-1, keepdims=True)
    log_total = row_max[..., 0] + jnp.log(jnp.sum(jnp.exp(scores - row_max), axis=-1))
    prob_out = jnp.exp(scores - log_total[..., None])
    part_out = jnp.einsum(
        "abqhk,khd->abqhd",
        prob_out.astype(jnp.bfloat16),
        value_rows,
        preferred_element_type=jnp.float32,
    ).astype(jnp.bfloat16)
    item_part = part_out.reshape(lead + (local_width,))
    item_query = recv_query.reshape(dp_count, capacity, span_len, heads_here, HEAD)
    prob_half = prob_out.astype(jnp.bfloat16)
    back_part, back_log = (
        lax.all_to_all(
            item_part.astype(jnp.float32), "dp", split_axis=0, concat_axis=0, tiled=True
        ).astype(item_part.dtype),
        lax.all_to_all(log_total, "dp", split_axis=0, concat_axis=0, tiled=True),
    )
    back_part = back_part.reshape(buffer_rows, span_len, local_width)
    back_log = back_log.reshape(buffer_rows, span_len, heads_here)
    got_part = back_part[position].reshape(spans, neigh, span_len, heads_here, HEAD)
    got_log = back_log[position].reshape(spans, neigh, span_len, heads_here)
    is_valid = jnp.arange(neigh, dtype=jnp.int32)[None, :] < counts[:, None]
    live = is_valid[:, :, None, None]
    masked = jnp.where(live, got_log, -1e30)
    top_part = jnp.max(masked, axis=1, keepdims=True)
    raw_weight = jnp.where(live, jnp.exp(masked - top_part), 0.0)
    mix_weight = raw_weight / jnp.sum(raw_weight, axis=1, keepdims=True)
    part_full = got_part.astype(jnp.float32)
    mixed_rows = jnp.sum(mix_weight[..., None] * part_full, axis=1)
    context = mixed_rows.astype(jnp.bfloat16).reshape(spans * span_len, local_width)
    grad_rows = cotangent.astype(jnp.float32).reshape(spans, span_len, heads_here, HEAD)
    part_grad = lax.optimization_barrier(
        (mix_weight[..., None] * grad_rows[:, None]).astype(jnp.bfloat16)
    )
    lse_grad = mix_weight * jnp.sum(grad_rows[:, None] * (part_full - mixed_rows[:, None]), axis=-1)
    rest_term = jnp.sum(part_grad.astype(jnp.float32) * part_full, axis=-1) - lse_grad
    send_grad = jnp.dot(
        place_half,
        part_grad.reshape(slots, span_len * local_width),
        preferred_element_type=jnp.float32,
    ).astype(jnp.bfloat16)
    send_grad = send_grad.reshape(dp_count, capacity, span_len, local_width)
    send_rest = jnp.dot(
        place_full, rest_term.reshape(slots, span_len * heads_here), precision=lax.Precision.HIGHEST
    )
    send_rest = send_rest.reshape(dp_count, capacity, span_len, heads_here)
    recv_grad, recv_rest = (
        lax.all_to_all(
            send_grad.astype(jnp.float32), "dp", split_axis=0, concat_axis=0, tiled=True
        ).astype(send_grad.dtype),
        lax.all_to_all(send_rest, "dp", split_axis=0, concat_axis=0, tiled=True),
    )
    item_grad = recv_grad.reshape(dp_count, capacity, span_len, heads_here, HEAD)
    dprob = jnp.einsum(
        "abqhd,khd->abqhk", item_grad, value_rows, preferred_element_type=jnp.float32
    )
    dscore = prob_out * (dprob - recv_rest[..., None])
    dscore_half = dscore.astype(jnp.bfloat16)
    item_dq = (
        jnp.einsum("abqhk,khd->abqhd", dscore_half, key_rows, preferred_element_type=jnp.float32)
        * score_scale
    )
    item_dq = item_dq.astype(jnp.bfloat16).reshape(dp_count, capacity, span_len, local_width)
    back_dq = lax.all_to_all(item_dq, "dp", split_axis=0, concat_axis=0, tiled=True)
    key_grad = (
        jnp.einsum("abqhk,abqhd->khd", dscore_half, item_query, preferred_element_type=jnp.float32)
        * score_scale
    )
    key_grad = key_grad.astype(jnp.bfloat16).reshape(nbr_dev * nbr_len, local_width)
    value_grad = jnp.einsum(
        "abqhk,abqhd->khd", prob_half, item_grad, preferred_element_type=jnp.float32
    )
    value_grad = value_grad.astype(jnp.bfloat16).reshape(nbr_dev * nbr_len, local_width)
    contract = (((1,), (1,)), ((), ()))
    state_term = lax.dot_general(key_grad, key_full, contract, preferred_element_type=jnp.float32)
    state_term = state_term + lax.dot_general(
        value_grad, value_full, contract, preferred_element_type=jnp.float32
    )
    summed = lax.psum_scatter(
        state_term.astype(jnp.bfloat16), "tensor", scatter_dimension=1, tiled=True
    ).astype(jnp.float32)
    state_grad = summed.astype(jnp.bfloat16).reshape(nbr_dev, nbr_len, summed.shape[1])
    got_dq = back_dq.reshape(buffer_rows, span_len * local_width)[position]
    got_dq = got_dq.reshape(spans, neigh, span_len * local_width).astype(jnp.float32)
    query_grad = jnp.sum(got_dq, axis=1).astype(jnp.bfloat16).reshape(spans * span_len, local_width)
    return (context, query_grad, state_grad)


def solution(mesh):
    placed = (
        P("dp", "tensor"),
        P("dp", None),
        P("dp"),
        P("dp", None, None),
        P("dp", "tensor"),
        P("dp", "tensor"),
        P("dp", "tensor"),
    )
    return jax.shard_map(
        local,
        mesh=mesh,
        in_specs=placed,
        out_specs=(P("dp", "tensor"), P("dp", "tensor"), P("dp", None, "tensor")),
        check_vma=False,
    )
```

profile of v0, /device:TPU:4, one launch (start us, length us, event | category | flops | bytes accessed | tf_op | source)
XLA Modules:
  0.0 683.3 jit_solution(17984772549266577789)
XLA Ops:
  12.6 3.6 copy.107
  16.2 12.4 %all-to-all-start = ((bf16[64,1,64,512]{3,2,1,0:T(8,128)(2,1)}), bf16[64,1,64,512]{3,2,1,0:T(8,128)(2,1)}, u32[]{:S(2)}, u32[]{:S(2)}) async-start(bf16[64,1,64,512]{3,2,1,0:T(8,128)(2,1)} %bitcast.204), calls=%async_computation | async-start | bytes 8388608 | tf_op jit(solution)/shard_map/all_to_all | solution.py:46
  29.3 106.6 %all-to-all-done = bf16[64,1,64,512]{3,2,1,0:T(8,128)(2,1)} async-done(((bf16[64,1,64,512]{3,2,1,0:T(8,128)(2,1)}), bf16[64,1,64,512]{3,2,1,0:T(8,128)(2,1)}, u32[]{:S(2)}, u32[]{:S(2)}) %all-to-all-start) | async-done | bytes 4194336 | tf_op jit(solution)/shard_map/all_to_all | solution.py:46
  135.9 6.9 %reshape.264 = bf16[64,64,4,128]{3,2,1,0:T(4,128)(2,1)} reshape(bf16[64,1,64,512]{3,2,1,0:T(8,128)(2,1)} %all-to-all-done) | data formatting | bytes 8388608 | tf_op jit(solution)/shard_map/reshape
  142.8 5.3 copy.81
  156.1 4.8 fusion.2
  161.7 6.9 %all-to-all-start.1 = ((f32[64,1,256]{2,1,0:T(1,128)}), f32[64,1,256]{2,1,0:T(1,128)S(1)}, u32[]{:S(2)}, u32[]{:S(2)}) async-start(f32[64,1,256]{2,1,0:T(1,128)} %reshape.325), calls=%async_computation.1 | async-start | bytes 131072 | tf_op jit(solution)/shard_map/all_to_all | solution.py:69
  168.7 6.9 %fusion.4 = bf16[64,1,64,4,128]{4,2,0,3,1:T(8,128)(2,1)} fusion(f32[64,64,4]{1,0,2:T(8,128)S(1)} %log_add_fusion, f32[4,128,4096]{1,2,0} %copy-done.2), kind=kLoop, calls=%fused_computation.15 | loop fusion | flops 6291456 | bytes 12648448 | tf_op jit(solution)/shard_map/convert_element_type | solution.py:58
  175.6 19.9 %all-gather.5.cloned.1.call-done = bf16[4096,512]{1,0:T(8,128)(2,1)} async-done(((bf16[64,512]{1,0:T(8,128)(2,1)}), bf16[4096,512]{1,0:T(8,128)(2,1)}) %all-gather.5.cloned.1.call-update) | async-done | bytes 4194320 | tf_op jit(solution)/shard_map/all_gather | solution.py:40
  200.1 4.1 convert_bitcast_fusion
  204.2 14.6 %copy.86 = f32[64,1,64,4,128]{4,3,1,2,0:T(4,128)} copy(f32[64,1,64,4,128]{4,2,0,3,1:T(8,128)} %convert_bitcast_fusion) | data formatting | bytes 16777216 | tf_op jit(solution)/shard_map/convert_element_type | solution.py:67
  218.7 8.1 %convert_bitcast_fusion.1 = bf16[64,64,1,512]{3,2,1,0:T(2,128)(2,1)} fusion(f32[64,1,64,512]{3,1,2,0:T(1,128)} %bitcast.197), kind=kLoop, calls=%fused_computation.76 | loop fusion | flops 2097152 | bytes 12582912
  227.4 28.4 %reduce.4 = bf16[64,64,512]{2,1,0:T(8,128)(2,1)} reduce(bf16[64,64,1,512]{3,2,1,0:T(2,128)(2,1)} %convert_bitcast_fusion.1, bf16[]{:T(256)} %broadcast.138), dimensions={2}, to_apply=%convert_bitcast_fusion.1.reduce_sub_computation | reduce | bytes 8388610
  255.7 7.8 %reshape.323 = bf16[64,2,16384]{2,1,0:T(2,128)(2,1)} reshape(bf16[64,64,512]{2,1,0:T(8,128)(2,1)} %reduce.4) | data formatting | bytes 8388608
  263.6 7.6 %all-to-all-start.2 = ((bf16[64,2,16384]{2,1,0:T(2,128)(2,1)}), bf16[64,2,16384]{2,1,0:T(2,128)(2,1)}, u32[]{:S(2)}, u32[]{:S(2)}) async-start(bf16[64,2,16384]{2,1,0:T(2,128)(2,1)} %reshape.323), calls=%async_computation.2 | async-start | bytes 8388608 | tf_op jit(solution)/shard_map/all_to_all | solution.py:66
  279.0 88.4 %all-to-all-done.2 = bf16[64,2,16384]{2,1,0:T(2,128)(2,1)} async-done(((bf16[64,2,16384]{2,1,0:T(2,128)(2,1)}), bf16[64,2,16384]{2,1,0:T(2,128)(2,1)}, u32[]{:S(2)}, u32[]{:S(2)}) %all-to-all-start.2) | async-done | bytes 4194336 | tf_op jit(solution)/shard_map/all_to_all | solution.py:66
  367.4 19.7 %reshape.324 = bf16[64,64,1,512]{3,2,1,0:T(2,128)(2,1)} reshape(bf16[64,2,16384]{2,1,0:T(2,128)(2,1)} %all-to-all-done.2) | data formatting | bytes 8388608
  387.1 6.9 %copy.138 = bf16[64,1,64,512]{3,2,1,0:T(8,128)(2,1)} copy(bf16[64,1,64,512]{3,1,2,0:T(2,128)(2,1)} %bitcast.196) | data formatting | bytes 8388608
  397.6 5.2 multiply_convert_fusion.2
  405.4 4.8 multiply_reduce_fusion
  415.6 5.5 all-to-all-start.4
  423.7 3.6 copy.109
  427.3 3.8 all-to-all-done.4
  431.1 6.9 %all-to-all-start.3 = ((bf16[64,1,64,512]{3,2,1,0:T(8,128)(2,1)}), bf16[64,1,64,512]{3,2,1,0:T(8,128)(2,1)}, u32[]{:S(2)}, u32[]{:S(2)}) async-start(bf16[64,1,64,512]{3,2,1,0:T(8,128)(2,1)} %bitcast.203), calls=%async_computation.3 | async-start | bytes 8388608 | tf_op jit(solution)/shard_map/all_to_all | solution.py:101
  438.9 95.3 %all-to-all-done.3 = bf16[64,1,64,512]{3,2,1,0:T(8,128)(2,1)} async-done(((bf16[64,1,64,512]{3,2,1,0:T(8,128)(2,1)}), bf16[64,1,64,512]{3,2,1,0:T(8,128)(2,1)}, u32[]{:S(2)}, u32[]{:S(2)}) %all-to-all-start.3) | async-done | bytes 4194336 | tf_op jit(solution)/shard_map/all_to_all | solution.py:101
  534.2 6.9 %reshape.272 = bf16[64,64,4,128]{3,2,1,0:T(4,128)(2,1)} reshape(bf16[64,1,64,512]{3,2,1,0:T(8,128)(2,1)} %all-to-all-done.3) | data formatting | bytes 8388608 | tf_op jit(solution)/shard_map/reshape.6
  547.8 5.1 multiply_convert_fusion.1
  558.2 5.7 all-to-all-start.5
  564.3 5.0 fusion.20
  577.5 82.6 %all-to-all-done.5 = bf16[64,1,64,512]{3,2,1,0:T(8,128)(2,1)} async-done(((bf16[64,1,64,512]{3,2,1,0:T(8,128)(2,1)}), bf16[64,1,64,512]{3,2,1,0:T(8,128)(2,1)}, u32[]{:S(2)}, u32[]{:S(2)}) %all-to-all-start.5) | async-done | bytes 4194336 | tf_op jit(solution)/shard_map/all_to_all | solution.py:117
  660.1 6.7 copy.110
  666.8 5.0 gather_fusion.2
  (104 shorter events, 68.1 us)
Async XLA Ops:
  7.2 140.9 %copy-start = (bf16[1,128,4096]{2,1,0:T(8,128)(2,1)S(1)}, bf16[1,128,4096]{2,1,0:T(8,128)(2,1)}, u32[]{:S(2)}) copy-start(bf16[1,128,4096]{2,1,0:T(8,128)(2,1)} %param.10) | copy-start | bytes 3145732
  7.2 140.9 %all-gather.3.cloned.1.call-start = ((), (), s32[]{:S(2)}) async-start(), calls=%async_computation.7 | async-start | bytes 4259840 | tf_op jit(solution)/shard_map/all_gather | solution.py:39
  8.9 3.7 copy-start.13
  16.2 119.7 %all-to-all-start = ((bf16[64,1,64,512]{3,2,1,0:T(8,128)(2,1)}), bf16[64,1,64,512]{3,2,1,0:T(8,128)(2,1)}, u32[]{:S(2)}, u32[]{:S(2)}) async-start(bf16[64,1,64,512]{3,2,1,0:T(8,128)(2,1)} %bitcast.204), calls=%async_computation | async-start | bytes 8388608 | tf_op jit(solution)/shard_map/all_to_all | solution.py:46
  28.6 166.9 %all-gather.5.cloned.1.call-start = ((), (), s32[]{:S(2)}) async-start(), calls=%async_computation.8 | async-start | bytes 4259840 | tf_op jit(solution)/shard_map/all_gather | solution.py:40
  148.1 3.5 copy-start.7
  152.8 3.2 copy-start.2
  161.7 101.8 %all-to-all-start.1 = ((f32[64,1,256]{2,1,0:T(1,128)}), f32[64,1,256]{2,1,0:T(1,128)S(1)}, u32[]{:S(2)}, u32[]{:S(2)}) async-start(f32[64,1,256]{2,1,0:T(1,128)} %reshape.325), calls=%async_computation.1 | async-start | bytes 131072 | tf_op jit(solution)/shard_map/all_to_all | solution.py:69
  195.4 3.4 copy-start.4
  263.5 7.7 %copy-start.11 = (bf16[512,512]{1,0:T(8,128)(2,1)S(1)}, bf16[512,512]{1,0:T(8,128)(2,1)}, u32[]{:S(2)}) copy-start(bf16[512,512]{1,0:T(8,128)(2,1)} %param.13) | copy-start | bytes 1572868
  263.5 9.1 %copy-start.14 = (s32[8]{0:T(128)S(1)}, s32[8]{0:T(128)}, u32[]{:S(2)}) copy-start(s32[8]{0:T(128)} %param.9) | copy-start | bytes 100
  263.6 103.8 %all-to-all-start.2 = ((bf16[64,2,16384]{2,1,0:T(2,128)(2,1)}), bf16[64,2,16384]{2,1,0:T(2,128)(2,1)}, u32[]{:S(2)}, u32[]{:S(2)}) async-start(bf16[64,2,16384]{2,1,0:T(2,128)(2,1)} %reshape.323), calls=%async_computation.2 | async-start | bytes 8388608 | tf_op jit(solution)/shard_map/all_to_all | solution.py:66
  273.3 120.7 %copy-start.12 = (s32[1024]{0:T(1024)}, s32[1024]{0:T(1024)S(1)}, u32[]{:S(2)}) copy-start(s32[1024]{0:T(1024)S(1)} %pad_clamp_fusion) | copy-start | bytes 12292
  415.6 15.5 %all-to-all-start.4 = ((f32[64,1,256]{2,1,0:T(1,128)}), f32[64,1,256]{2,1,0:T(1,128)S(1)}, u32[]{:S(2)}, u32[]{:S(2)}) async-start(f32[64,1,256]{2,1,0:T(1,128)} %reshape.327), calls=%async_computation.4 | async-start | bytes 131072 | tf_op jit(solution)/shard_map/all_to_all | solution.py:104
  431.1 103.1 %all-to-all-start.3 = ((bf16[64,1,64,512]{3,2,1,0:T(8,128)(2,1)}), bf16[64,1,64,512]{3,2,1,0:T(8,128)(2,1)}, u32[]{:S(2)}, u32[]{:S(2)}) async-start(bf16[64,1,64,512]{3,2,1,0:T(8,128)(2,1)} %bitcast.203), calls=%async_computation.3 | async-start | bytes 8388608 | tf_op jit(solution)/shard_map/all_to_all | solution.py:101
  544.4 3.4 copy-start.3
  552.9 2.0 copy-start.6
  558.2 101.9 %all-to-all-start.5 = ((bf16[64,1,64,512]{3,2,1,0:T(8,128)(2,1)}), bf16[64,1,64,512]{3,2,1,0:T(8,128)(2,1)}, u32[]{:S(2)}, u32[]{:S(2)}) async-start(bf16[64,1,64,512]{3,2,1,0:T(8,128)(2,1)} %bitcast_bitcast_fusion), calls=%async_computation.5 | async-start | bytes 8388608 | tf_op jit(solution)/shard_map/all_to_all | solution.py:117
  563.9 112.7 %reduce-scatter.2.cloned.1.call-start = ((), (), s32[]{:S(2)}) async-start(), calls=%async_computation.9 | async-start | bytes 1310720 | tf_op jit(solution)/shard_map/reduce_scatter | solution.py:132
  564.3 5.0 copy-start.9
  564.3 6.5 copy-start.10
  569.3 2.4 copy-start.5
  571.7 2.2 copy-start.8
  666.8 9.8 %copy-start.1 = (bf16[1,128,4096]{2,1,0:T(8,128)(2,1)S(1)}, bf16[1,128,4096]{2,1,0:T(8,128)(2,1)}, u32[]{:S(2)}) copy-start(bf16[1,128,4096]{2,1,0:T(8,128)(2,1)} %param.10) | copy-start | bytes 3145732
Sparse Core Ops, SparseCore 0:
  10.8 103.1 all-gather.2
  116.7 78.6 all-gather.4
  576.6 25.5 reduce-scatter.1
where the time goes:
time: 694 us; the launch traced here: 683 us
  waiting for transfers between devices  398 us (57%)
  local copies, waits for them, and re-layouts  119 us (17%)
  other arithmetic  79.9 us (12%)
  starting transfers between devices  45.4 us (7%)
  matrix products  26.4 us (4%)
  between operations  14.4 us (2%)
    all_to_all x1, waiting for transfers between devices, local(): lax.all_to_all(send_query, 'dp', split_axis=0, concat_axis=0, tiled=True)  107 us
    all_to_all x1, waiting for transfers between devices, local(): lax.all_to_all(send_grad.astype(jnp.float32), 'dp', split_axis=0, concat_...  95.3 us
    all_to_all x1, waiting for transfers between devices, local(): lax.all_to_all(item_part.astype(jnp.float32), 'dp', split_axis=0, concat_...  88.4 us
    all_to_all x1, waiting for transfers between devices, local(): lax.all_to_all(item_dq, 'dp', split_axis=0, concat_axis=0, tiled=True)  82.6 us
    unnamed x43, local copies, waits for them, and re-layouts  58.6 us
    unnamed x2, other arithmetic  36.5 us
    all_gather x1, waiting for transfers between devices, local(): value_full = lax.all_gather(w_value, 'dp', axis=0, tiled=True)  19.9 us
    convert_element_type x1, local copies, waits for them, and re-layouts, local(): item_part.astype(jnp.float32)  14.6 us
  transfers between devices with their start and end apart: 9, of which 6 were waited for; matrix products, arithmetic and copies ran while one was open for 22% of the time, Pallas kernels for 0%

commit v1 on v0

--- a/solution.py
+++ b/solution.py
@@ -5,6 +5,14 @@
 from jax.sharding import PartitionSpec as P
 
 HEAD = 128
+
+
+def _wait_limits(own_rows, device_axis, d0):
+    x_now = lax.psum(1, device_axis)
+    part_next = jnp.stack([own_rows] * x_now, axis=0)
+    mid_arr = lax.all_to_all(part_next, device_axis, 0, 0)
+    tile_out = jnp.concatenate(mid_arr, d0)
+    return tile_out
 
 
 def local(queries, neighbours, counts, states, w_key, w_value, cotangent):
@@ -37,7 +45,7 @@
     send_query = send_query.reshape(dp_count, capacity, span_len, local_width)
     flat_states = states.reshape(nbr_dev * nbr_len, dmodel)
     key_full = lax.all_gather(w_key, "dp", axis=0, tiled=True)
-    value_full = lax.all_gather(w_value, "dp", axis=0, tiled=True)
+    value_full = _wait_limits(w_value, "dp", 0)
     key_acc = jnp.dot(flat_states, key_full, preferred_element_type=jnp.float32)
     value_acc = jnp.dot(flat_states, value_full, preferred_element_type=jnp.float32)
     key_rows = key_acc.astype(jnp.bfloat16).reshape(nbr_len, heads_here, HEAD)

time: 694 us -> 745 us (1.073)
  waiting for transfers between devices: 398 us -> 441 us
  starting transfers between devices: 45.4 us -> 53.5 us
    all_to_all x0 -> x1, waiting for transfers between devices: none -> 63.5 us  [_wait_limits(): mid_arr = lax.all_to_all(part_next, device_axis, 0, 0)]
    all_gather x1 -> x0, waiting for transfers between devices: 19.9 us -> none  [local(): value_full = lax.all_gather(w_value, 'dp', axis=0, tiled=True)]
  transfers between devices with their start and end apart: 9 -> 9, of which waited for: 6 -> 6; matrix products, arithmetic and copies ran while one was open for 22% -> 20% of each run, Pallas kernels for 0% -> 0%
where the time goes in v1:
time: 745 us; the launch traced here: 738 us
  waiting for transfers between devices  441 us (59%)
  local copies, waits for them, and re-layouts  121 us (16%)
  other arithmetic  79.9 us (11%)
  starting transfers between devices  53.5 us (7%)
  matrix products  28.5 us (4%)
  between operations  14.7 us (2%)
    all_to_all x1, waiting for transfers between devices, local(): lax.all_to_all(send_query, 'dp', split_axis=0, concat_axis=0, tiled=True)  108 us
    all_to_all x1, waiting for transfers between devices, local(): lax.all_to_all(send_grad.astype(jnp.float32), 'dp', split_axis=0, concat_...  95.3 us
    all_to_all x1, waiting for transfers between devices, local(): lax.all_to_all(item_part.astype(jnp.float32), 'dp', split_axis=0, concat_...  88.4 us
    all_to_all x1, waiting for transfers between devices, local(): lax.all_to_all(item_dq, 'dp', split_axis=0, concat_axis=0, tiled=True)  81.2 us
    all_to_all x1, waiting for transfers between devices, _wait_limits(): mid_arr = lax.all_to_all(part_next, device_axis, 0, 0)  63.5 us
    unnamed x43, local copies, waits for them, and re-layouts  57.7 us
    unnamed x2, other arithmetic  36.5 us
  transfers between devices with their start and end apart: 9, of which 6 were waited for; matrix products, arithmetic and copies ran while one was open for 20% of the time, Pallas kernels for 0%

profile of v1, /device:TPU:4, one launch (start us, length us, event | category | flops | bytes accessed | tf_op | source)
XLA Modules:
  0.0 738.4 jit_solution(7751668628842555635)
XLA Ops:
  15.5 12.5 %all-to-all-start = ((bf16[64,1,64,512]{3,2,1,0:T(8,128)(2,1)}), bf16[64,1,64,512]{3,2,1,0:T(8,128)(2,1)}, u32[]{:S(2)}, u32[]{:S(2)}) async-start(bf16[64,1,64,512]{3,2,1,0:T(8,128)(2,1)} %bitcast.205), calls=%async_computation | async-start | bytes 8388608 | tf_op jit(solution)/shard_map/all_to_all | solution.py:54
  28.7 107.8 %all-to-all-done = bf16[64,1,64,512]{3,2,1,0:T(8,128)(2,1)} async-done(((bf16[64,1,64,512]{3,2,1,0:T(8,128)(2,1)}), bf16[64,1,64,512]{3,2,1,0:T(8,128)(2,1)}, u32[]{:S(2)}, u32[]{:S(2)}) %all-to-all-start) | async-done | bytes 4194336 | tf_op jit(solution)/shard_map/all_to_all | solution.py:54
  139.0 6.0 all-to-all-start.2
  144.9 6.9 reshape.269
  151.9 5.3 copy.81
  165.1 4.8 fusion.2
  170.8 6.9 fusion.4
  177.7 63.5 %all-to-all-done.2 = bf16[64,64,512]{2,1,0:T(8,128)(2,1)} async-done(((bf16[64,64,512]{2,1,0:T(8,128)(2,1)}), bf16[64,64,512]{2,1,0:T(8,128)(2,1)}, u32[]{:S(2)}, u32[]{:S(2)}) %all-to-all-start.2) | async-done | bytes 4194336 | tf_op jit(solution)/shard_map/all_to_all | solution.py:13
  241.2 5.8 all-to-all-start.1
  251.6 4.1 convert_bitcast_fusion
  255.7 14.6 %copy.86 = f32[64,1,64,4,128]{4,3,1,2,0:T(4,128)} copy(f32[64,1,64,4,128]{4,2,0,3,1:T(8,128)} %convert_bitcast_fusion) | data formatting | bytes 16777216 | tf_op jit(solution)/shard_map/convert_element_type | solution.py:75
  270.3 8.0 %convert_bitcast_fusion.1 = bf16[64,64,1,512]{3,2,1,0:T(2,128)(2,1)} fusion(f32[64,1,64,512]{3,1,2,0:T(1,128)} %bitcast.198), kind=kLoop, calls=%fused_computation.76 | loop fusion | flops 2097152 | bytes 12582912
  278.7 28.5 %reduce.4 = bf16[64,64,512]{2,1,0:T(8,128)(2,1)} reduce(bf16[64,64,1,512]{3,2,1,0:T(2,128)(2,1)} %convert_bitcast_fusion.1, bf16[]{:T(256)} %broadcast.140), dimensions={2}, to_apply=%convert_bitcast_fusion.1.reduce_sub_computation | reduce | bytes 8388610
  307.3 7.8 %reshape.329 = bf16[64,2,16384]{2,1,0:T(2,128)(2,1)} reshape(bf16[64,64,512]{2,1,0:T(8,128)(2,1)} %reduce.4) | data formatting | bytes 8388608
  315.1 10.8 %all-to-all-start.3 = ((bf16[64,2,16384]{2,1,0:T(2,128)(2,1)}), bf16[64,2,16384]{2,1,0:T(2,128)(2,1)}, u32[]{:S(2)}, u32[]{:S(2)}) async-start(bf16[64,2,16384]{2,1,0:T(2,128)(2,1)} %reshape.329), calls=%async_computation.3 | async-start | bytes 8388608 | tf_op jit(solution)/shard_map/all_to_all | solution.py:74
  333.7 88.4 %all-to-all-done.3 = bf16[64,2,16384]{2,1,0:T(2,128)(2,1)} async-done(((bf16[64,2,16384]{2,1,0:T(2,128)(2,1)}), bf16[64,2,16384]{2,1,0:T(2,128)(2,1)}, u32[]{:S(2)}, u32[]{:S(2)}) %all-to-all-start.3) | async-done | bytes 4194336 | tf_op jit(solution)/shard_map/all_to_all | solution.py:74
  422.2 19.7 %reshape.330 = bf16[64,64,1,512]{3,2,1,0:T(2,128)(2,1)} reshape(bf16[64,2,16384]{2,1,0:T(2,128)(2,1)} %all-to-all-done.3) | data formatting | bytes 8388608
  441.9 6.9 copy.138
  452.3 5.2 multiply_convert_fusion.2
  460.2 4.8 multiply_reduce_fusion
  470.4 5.5 all-to-all-start.5
  482.1 3.8 all-to-all-done.5
  485.9 6.9 all-to-all-start.4
  493.7 95.3 %all-to-all-done.4 = bf16[64,1,64,512]{3,2,1,0:T(8,128)(2,1)} async-done(((bf16[64,1,64,512]{3,2,1,0:T(8,128)(2,1)}), bf16[64,1,64,512]{3,2,1,0:T(8,128)(2,1)}, u32[]{:S(2)}, u32[]{:S(2)}) %all-to-all-start.4) | async-done | bytes 4194336 | tf_op jit(solution)/shard_map/all_to_all | solution.py:109
  589.0 6.9 reshape.278
  602.6 5.1 multiply_convert_fusion.1
  613.0 5.7 all-to-all-start.6
  619.1 5.0 fusion.20
  627.9 4.7 fusion.5
  633.7 81.2 %all-to-all-done.6 = bf16[64,1,64,512]{3,2,1,0:T(8,128)(2,1)} async-done(((bf16[64,1,64,512]{3,2,1,0:T(8,128)(2,1)}), bf16[64,1,64,512]{3,2,1,0:T(8,128)(2,1)}, u32[]{:S(2)}, u32[]{:S(2)}) %all-to-all-start.6) | async-done | bytes 4194336 | tf_op jit(solution)/shard_map/all_to_all | solution.py:125
  714.9 6.6 copy.110
  721.5 5.0 gather_fusion.2
  (104 shorter events, 73.8 us)
Async XLA Ops:
  7.2 150.0 %copy-start = (bf16[1,128,4096]{2,1,0:T(8,128)(2,1)S(1)}, bf16[1,128,4096]{2,1,0:T(8,128)(2,1)}, u32[]{:S(2)}) copy-start(bf16[1,128,4096]{2,1,0:T(8,128)(2,1)} %param.10) | copy-start | bytes 3145732
  8.3 3.7 copy-start.13
  15.5 121.0 %copy-start.11 = (bf16[64,512]{1,0:T(8,128)(2,1)S(1)}, bf16[64,512]{1,0:T(8,128)(2,1)}, u32[]{:S(2)}) copy-start(bf16[64,512]{1,0:T(8,128)(2,1)} %param.12) | copy-start | bytes 196612
  15.5 121.0 %all-to-all-start = ((bf16[64,1,64,512]{3,2,1,0:T(8,128)(2,1)}), bf16[64,1,64,512]{3,2,1,0:T(8,128)(2,1)}, u32[]{:S(2)}, u32[]{:S(2)}) async-start(bf16[64,1,64,512]{3,2,1,0:T(8,128)(2,1)} %bitcast.205), calls=%async_computation | async-start | bytes 8388608 | tf_op jit(solution)/shard_map/all_to_all | solution.py:54
  28.0 129.2 %all-gather.2.cloned.1.call-start = ((), (), s32[]{:S(2)}) async-start(), calls=%async_computation.8 | async-start | bytes 4259840 | tf_op jit(solution)/shard_map/all_gather | solution.py:47
  139.0 102.2 %all-to-all-start.2 = ((bf16[64,64,512]{2,1,0:T(8,128)(2,1)}), bf16[64,64,512]{2,1,0:T(8,128)(2,1)}, u32[]{:S(2)}, u32[]{:S(2)}) async-start(bf16[64,64,512]{2,1,0:T(8,128)(2,1)} %stack.2), calls=%async_computation.2 | async-start | bytes 8388608 | tf_op jit(solution)/shard_map/all_to_all | solution.py:13
  157.2 3.5 copy-start.7
  161.9 3.2 copy-start.2
  241.2 73.9 %all-to-all-start.1 = ((f32[64,1,256]{2,1,0:T(1,128)}), f32[64,1,256]{2,1,0:T(1,128)S(1)}, u32[]{:S(2)}, u32[]{:S(2)}) async-start(f32[64,1,256]{2,1,0:T(1,128)} %reshape.331), calls=%async_computation.1 | async-start | bytes 131072 | tf_op jit(solution)/shard_map/all_to_all | solution.py:77
  247.0 3.5 copy-start.4
  315.1 10.9 %copy-start.10 = (bf16[512,512]{1,0:T(8,128)(2,1)S(1)}, bf16[512,512]{1,0:T(8,128)(2,1)}, u32[]{:S(2)}) copy-start(bf16[512,512]{1,0:T(8,128)(2,1)} %param.13) | copy-start | bytes 1572868
  315.1 12.3 %copy-start.14 = (s32[8]{0:T(128)S(1)}, s32[8]{0:T(128)}, u32[]{:S(2)}) copy-start(s32[8]{0:T(128)} %param.9) | copy-start | bytes 100
  315.1 107.0 %all-to-all-start.3 = ((bf16[64,2,16384]{2,1,0:T(2,128)(2,1)}), bf16[64,2,16384]{2,1,0:T(2,128)(2,1)}, u32[]{:S(2)}, u32[]{:S(2)}) async-start(bf16[64,2,16384]{2,1,0:T(2,128)(2,1)} %reshape.329), calls=%async_computation.3 | async-start | bytes 8388608 | tf_op jit(solution)/shard_map/all_to_all | solution.py:74
  328.1 120.7 %copy-start.12 = (s32[1024]{0:T(1024)}, s32[1024]{0:T(1024)S(1)}, u32[]{:S(2)}) copy-start(s32[1024]{0:T(1024)S(1)} %pad_clamp_fusion) | copy-start | bytes 12292
  470.4 15.5 %all-to-all-start.5 = ((f32[64,1,256]{2,1,0:T(1,128)}), f32[64,1,256]{2,1,0:T(1,128)S(1)}, u32[]{:S(2)}, u32[]{:S(2)}) async-start(f32[64,1,256]{2,1,0:T(1,128)} %reshape.333), calls=%async_computation.5 | async-start | bytes 131072 | tf_op jit(solution)/shard_map/all_to_all | solution.py:112
  485.9 103.1 %all-to-all-start.4 = ((bf16[64,1,64,512]{3,2,1,0:T(8,128)(2,1)}), bf16[64,1,64,512]{3,2,1,0:T(8,128)(2,1)}, u32[]{:S(2)}, u32[]{:S(2)}) async-start(bf16[64,1,64,512]{3,2,1,0:T(8,128)(2,1)} %bitcast.204), calls=%async_computation.4 | async-start | bytes 8388608 | tf_op jit(solution)/shard_map/all_to_all | solution.py:109
  599.2 3.4 copy-start.3
  607.7 2.0 copy-start.6
  613.0 101.9 %all-to-all-start.6 = ((bf16[64,1,64,512]{3,2,1,0:T(8,128)(2,1)}), bf16[64,1,64,512]{3,2,1,0:T(8,128)(2,1)}, u32[]{:S(2)}, u32[]{:S(2)}) async-start(bf16[64,1,64,512]{3,2,1,0:T(8,128)(2,1)} %bitcast_bitcast_fusion), calls=%async_computation.6 | async-start | bytes 8388608 | tf_op jit(solution)/shard_map/all_to_all | solution.py:125
  618.7 112.7 %reduce-scatter.2.cloned.1.call-start = ((), (), s32[]{:S(2)}) async-start(), calls=%async_computation.9 | async-start | bytes 1310720 | tf_op jit(solution)/shard_map/reduce_scatter | solution.py:140
  619.1 5.0 copy-start.8
  619.1 6.5 copy-start.9
  624.1 2.4 copy-start.5
  721.5 9.8 %copy-start.1 = (bf16[1,128,4096]{2,1,0:T(8,128)(2,1)S(1)}, bf16[1,128,4096]{2,1,0:T(8,128)(2,1)}, u32[]{:S(2)}) copy-start(bf16[1,128,4096]{2,1,0:T(8,128)(2,1)} %param.10) | copy-start | bytes 3145732
Sparse Core Ops, SparseCore 0:
  31.6 96.6 all-gather.1
  632.7 25.5 reduce-scatter.1
